TPU v7x, 32 devices: a whole 2x2x4 slice. The times are simulated.
32 devices in a mesh: seq: 8 (over z, x), head: 2 (over y), enc: 2 (over core).
Axes of the slice: x: 2, y: 2, z: 4, core: 2. Of those that a mesh axis runs over, the one named last changes fastest.
Arguments:
- queries: bfloat16 [2560, 1024], P('seq', ('head', 'enc')), may hold values from -2000 to 2000
- keys: bfloat16 [2560, 1024], P('seq', ('head', 'enc')), may hold values from -2000 to 2000
- values: bfloat16 [2560, 1024], P('seq', ('head', 'enc')), may hold values from -6 to 6
- out_weight: bfloat16 [1024, 5120], P(('head', 'enc'), 'seq'), may hold values from -0.25 to 0.25
- q_gain: float32 [1024], P(('head', 'enc')), may hold values from 0.75 to 3
- k_gain: float32 [1024], P(('head', 'enc')), may hold values from 0.75 to 3
- gate: float32 [5120], P(('head', 'enc')), may hold values from 1 to 8
- valid_count: int32 [1], replicated, may hold values from 1280 to 2560
Outputs:
- update: bfloat16 [2560, 5120], P('seq', ('head', 'enc'))
Inputs may be any that keep to these rules, and one draw needn't show every extreme that they name: Key positions from valid_count[0] on are padding and take no weight.
All inputs are finite; a program needn't handle non-finite values.
Results may differ from a plain program's by a relative error of at most 0.015.
The roundings to bfloat16 on the way count: a program that leaves them out, or rounds other values in their place, can miss the bound.
Values may be sent and summed in bfloat16 or wider, within the bound.
A program may use at most 64 MiB of HBM per device.

v0:
```python
import jax
import jax.numpy as jnp
from jax import lax
from jax.sharding import PartitionSpec as P

HEAD_DIM = 128


epsilon = 1e-06
lowest_score = -1e30


def normalize(matrix, squares, gain_row, feature_count):
    inverse_rms = lax.rsqrt(squares / feature_count + epsilon)
    return (matrix.astype(jnp.float32) * inverse_rms[:, None] * gain_row[None, :]).astype(
        jnp.bfloat16
    )


def absorb(carried, query_heads, key_block, value_block, offset, key_limit):
    running_sum, running_max, running_mass = carried
    scale_factor = query_heads.shape[2] ** (-0.5)
    scores = (
        jnp.einsum("qhd,khd->hqk", query_heads, key_block, preferred_element_type=jnp.float32)
        * scale_factor
    )
    position = offset + jnp.arange(key_block.shape[0], dtype=jnp.int32)
    usable = (position < key_limit)[None, None, :]
    masked = jnp.where(usable, scores, lowest_score)
    new_max = jnp.maximum(running_max, jnp.max(masked, axis=2))
    weights = jnp.where(usable, jnp.exp(masked - new_max[:, :, None]), 0.0)
    factor = jnp.exp(running_max - new_max)
    running_mass = running_mass * factor + jnp.sum(weights, axis=2)
    running_sum = running_sum * factor[:, :, None] + jnp.einsum(
        "hqk,khd->hqd",
        weights.astype(jnp.bfloat16),
        value_block,
        preferred_element_type=jnp.float32,
    )
    return (running_sum, new_max, running_mass)


def absorb_blocks(carried, query_heads, key_rows, value_rows, key_limit):
    row_total = key_rows.shape[0]
    block_size = 512
    block_count = row_total // block_size
    key_blocks = key_rows.reshape((block_count, block_size) + key_rows.shape[1:])
    value_blocks = value_rows.reshape((block_count, block_size) + value_rows.shape[1:])

    def absorb_block(running, triple):
        block_number, key_block, value_block = triple
        return (
            absorb(
                running, query_heads, key_block, value_block, block_number * block_size, key_limit
            ),
            None,
        )

    numbers = jnp.arange(block_count, dtype=jnp.int32)
    carried, _ = lax.scan(absorb_block, carried, (numbers, key_blocks, value_blocks))
    return carried


def visit(carried, query_heads, key_rows, value_rows, offset, key_limit):
    return lax.cond(
        offset < key_limit,
        lambda running: absorb_blocks(running, query_heads, key_rows, value_rows, key_limit),
        lambda running: running,
        carried,
    )


def local(queries, keys, values, out_weight, q_gain, k_gain, gate, valid_count):
    row_count = queries.shape[0]
    local_heads = queries.shape[1] // HEAD_DIM
    feature_count = queries.shape[1] * lax.axis_size(("head", "enc"))
    key_limit = valid_count[0]
    query_squares = jnp.sum(jnp.square(queries.astype(jnp.float32)), axis=1)
    key_squares = jnp.sum(jnp.square(keys.astype(jnp.float32)), axis=1)
    query_totals, key_totals = lax.psum((query_squares, key_squares), ("head", "enc"))
    query_heads = normalize(queries, query_totals, q_gain, feature_count).reshape(
        row_count, local_heads, HEAD_DIM
    )
    key_heads = normalize(keys, key_totals, k_gain, feature_count).reshape(
        row_count, local_heads, HEAD_DIM
    )
    value_heads = values.reshape(row_count, local_heads, HEAD_DIM)
    initial = (
        jnp.zeros((local_heads, row_count, HEAD_DIM), jnp.float32),
        jnp.full((local_heads, row_count), lowest_score, jnp.float32),
        jnp.zeros((local_heads, row_count), jnp.float32),
    )
    running_sum, running_max, running_mass = visit(
        initial,
        query_heads,
        lax.all_gather(key_heads, "seq", axis=0, tiled=True),
        lax.all_gather(value_heads, "seq", axis=0, tiled=True),
        jnp.int32(0),
        key_limit,
    )
    attended = (running_sum / running_mass[:, :, None]).transpose(1, 0, 2)
    attended = attended.reshape(row_count, local_heads * HEAD_DIM).astype(jnp.bfloat16)
    terms = jnp.dot(
        attended,
        lax.all_gather(out_weight, "seq", axis=1, tiled=True),
        preferred_element_type=jnp.float32,
    )
    summed = lax.psum_scatter(
        terms.astype(jnp.bfloat16), ("head", "enc"), scatter_dimension=1, tiled=True
    ).astype(jnp.float32)
    return (gate[None, :] * summed).astype(jnp.bfloat16)


def solution(mesh):
    placed = (
        P("seq", ("head", "enc")),
        P("seq", ("head", "enc")),
        P("seq", ("head", "enc")),
        P(("head", "enc"), "seq"),
        P(("head", "enc")),
        P(("head", "enc")),
        P(("head", "enc")),
        P(),
    )
    return jax.shard_map(
        local, mesh=mesh, in_specs=placed, out_specs=P("seq", ("head", "enc")), check_vma=False
    )
```

profile of v0, /device:TPU:0, one launch (start us, length us, event | category | flops | bytes accessed | tf_op | source)
XLA Modules:
  0.0 209.7 jit_solution(12442245046292359948)
XLA Ops:
  6.5 1.2 fusion.11
  7.8 8.4 %all-reduce = (f32[320]{0:T(512)S(1)}, f32[320]{0:T(512)S(1)}) all-reduce(f32[320]{0:T(512)S(1)} %get-tuple-element.161, f32[320]{0:T(512)S(1)} %get-tuple-element.162), channel_id=1, replica_groups=mesh['seq'=8,'head'=2,'enc'=2] {'head','enc'}, use_global_device_ids=true, to_apply=%region_1.0 | all-reduce | flops 640 | bytes 5120 | tf_op jit(solution)/shard_map/psum | solution.py:80
  18.0 1.6 reshape.34
  21.2 39.0 %all-gather.4.cloned.1.call-done = bf16[2560,2,128]{2,1,0:T(2,128)(2,1)} async-done(((bf16[320,2,128]{2,1,0:T(2,128)(2,1)}), bf16[2560,2,128]{2,1,0:T(2,128)(2,1)}) %all-gather.4.cloned.1.call-update) | async-done | bytes 1310736 | tf_op jit(solution)/shard_map/all_gather | solution.py:96
  60.2 42.9 %all-gather.6.cloned.1.call-done = bf16[2560,2,128]{2,1,0:T(2,128)(2,1)} async-done(((bf16[320,2,128]{2,1,0:T(2,128)(2,1)}), bf16[2560,2,128]{2,1,0:T(2,128)(2,1)}) %all-gather.6.cloned.1.call-update) | async-done | bytes 1310736 | tf_op jit(solution)/shard_map/all_gather | solution.py:97
  103.1 36.4 %conditional.1 = (f32[2,320,128]{2,1,0:T(8,128)}, f32[2,320]{1,0:T(2,128)}) conditional(s32[]{:T(128)} %convert_element_type.38, () %tuple.17, (bf16[2560,2,128]{2,1,0:T(2,128)(2,1)}, bf16[2560,2,128]{2,1,0:T(2,128)(2,1)}, bf16[320,256]{1,0:T(8,128)(2,1)S(1)}, s32[]{:T(128)}) %tuple.18), branch_computations={%region_4.0_spmd, %region_5.10_spmd} | conditional | flops 170971264 | bytes 6695217 | solution.py:65
  103.1 36.3 %while.14 = (s32[]{:T(128)}, f32[2,320,128]{2,1,0:T(8,128)}, f32[2,320]{1,0:T(2,128)S(1)}, f32[2,320]{1,0:T(2,128)}, s32[5]{0:T(128)S(1)}, /*index=5*/s32[]{:T(1...) while((s32[]{:T(128)}, f32[2,320,128]{2,1,0:T(8,128)}, ...), condition=%wide.region_9.9_spmd.clone, body=%wide.region_6.8_spmd.clone.sunk | while | flops 170971264 | bytes 6367397 | solution.py:60
  105.1 1.4 constant_dynamic-slice_fusion.3
  111.0 1.4 constant_dynamic-slice_fusion.3
  113.3 1.3 fusion.37
  114.6 2.1 %convolution_add_fusion.2 = f32[2,320,128]{2,1,0:T(8,128)} fusion(f32[2,320,512]{2,1,0:T(8,128)S(1)} %get-tuple-element.225, f32[2,320]{1,0:T(2,128)S(1)} %fusion.35, pred[512]{0:T(512)(128)(4,1)S(1)} %add_compare_fusion.2, f32[2,320,128]{2,1,0:T(8,128)} %get-tuple-element.243, bf16[1,512,2,128]{3,2,1,0:T(2,128)(2,1)S(1)} %get-tuple-element.227, ...), kind=kOutput, calls=%fused_computation.4.clone.1 | convolution fusion | flops 85114880 | bytes 2233857 | tf_op jit(solution)/shard_map/cond/branch_1_fun/while/body/eval_jaxpr/hqk,khd->hqd/dot_general | solution.py:34
  118.7 1.4 constant_dynamic-slice_fusion.3
  120.9 1.3 fusion.37
  122.2 2.1 %convolution_add_fusion.2 = f32[2,320,128]{2,1,0:T(8,128)} fusion(f32[2,320,512]{2,1,0:T(8,128)S(1)} %get-tuple-element.225, f32[2,320]{1,0:T(2,128)S(1)} %fusion.35, pred[512]{0:T(512)(128)(4,1)S(1)} %add_compare_fusion.2, f32[2,320,128]{2,1,0:T(8,128)} %get-tuple-element.243, bf16[1,512,2,128]{3,2,1,0:T(2,128)(2,1)S(1)} %get-tuple-element.227, ...), kind=kOutput, calls=%fused_computation.4.clone.1 | convolution fusion | flops 85114880 | bytes 2233857 | tf_op jit(solution)/shard_map/cond/branch_1_fun/while/body/eval_jaxpr/hqk,khd->hqd/dot_general | solution.py:34
  126.3 1.4 constant_dynamic-slice_fusion.3
  128.5 1.3 fusion.37
  129.8 2.1 %convolution_add_fusion.2 = f32[2,320,128]{2,1,0:T(8,128)} fusion(f32[2,320,512]{2,1,0:T(8,128)S(1)} %get-tuple-element.225, f32[2,320]{1,0:T(2,128)S(1)} %fusion.35, pred[512]{0:T(512)(128)(4,1)S(1)} %add_compare_fusion.2, f32[2,320,128]{2,1,0:T(8,128)} %get-tuple-element.243, bf16[1,512,2,128]{3,2,1,0:T(2,128)(2,1)S(1)} %get-tuple-element.227, ...), kind=kOutput, calls=%fused_computation.4.clone.1 | convolution fusion | flops 85114880 | bytes 2233857 | tf_op jit(solution)/shard_map/cond/branch_1_fun/while/body/eval_jaxpr/hqk,khd->hqd/dot_general | solution.py:34
  133.8 1.4 constant_dynamic-slice_fusion.3
  136.1 1.3 fusion.37
  137.4 2.1 %convolution_add_fusion.2 = f32[2,320,128]{2,1,0:T(8,128)} fusion(f32[2,320,512]{2,1,0:T(8,128)S(1)} %get-tuple-element.225, f32[2,320]{1,0:T(2,128)S(1)} %fusion.35, pred[512]{0:T(512)(128)(4,1)S(1)} %add_compare_fusion.2, f32[2,320,128]{2,1,0:T(8,128)} %get-tuple-element.243, bf16[1,512,2,128]{3,2,1,0:T(2,128)(2,1)S(1)} %get-tuple-element.227, ...), kind=kOutput, calls=%fused_computation.4.clone.1 | convolution fusion | flops 85114880 | bytes 2233857 | tf_op jit(solution)/shard_map/cond/branch_1_fun/while/body/eval_jaxpr/hqk,khd->hqd/dot_general | solution.py:34
  139.5 19.6 %all-gather.8.cloned.1.call-done = bf16[256,5120]{1,0:T(8,128)(2,1)} async-done(((bf16[256,640]{1,0:T(8,128)(2,1)}), bf16[256,5120]{1,0:T(8,128)(2,1)}) %all-gather.8.cloned.1.call-update) | async-done | bytes 2621456 | tf_op jit(solution)/shard_map/all_gather | solution.py:105
  159.1 4.6 %convolution_convert_fusion = bf16[320,5120]{1,0:T(8,128)(2,1)} fusion(bf16[256,5120]{1,0:T(8,128)(2,1)} %all-gather.8.cloned.1.call-done, f32[2,320,128]{2,1,0:T(8,128)} %get-tuple-element.68, f32[2,320]{1,0:T(2,128)} %get-tuple-element.69), kind=kOutput, calls=%fused_computation.23 | convolution fusion | flops 840663040 | bytes 6228480 | tf_op jit(solution)/shard_map/dot_general | solution.py:103
  163.8 37.3 %reduce-scatter.2.cloned.1.call-done = bf16[320,1280]{1,0:T(8,128)(2,1)} async-done(((bf16[320,5120]{1,0:T(8,128)(2,1)}), bf16[320,1280]{1,0:T(8,128)(2,1)}) %reduce-scatter.2.cloned.1.call-update) | async-done | bytes 819216 | tf_op jit(solution)/shard_map/reduce_scatter | solution.py:108
  201.0 2.2 %multiply_convert_fusion = bf16[320,1280]{1,0:T(8,128)(2,1)} fusion(bf16[320,1280]{1,0:T(8,128)(2,1)} %reduce-scatter.2.cloned.1.call-done, f32[1280]{0:T(1024)S(1)} %copy-done.1), kind=kLoop, calls=%fused_computation.24 | loop fusion | flops 1228800 | bytes 1643520 | tf_op jit(solution)/shard_map/convert_element_type | solution.py:111
  (56 shorter events, 15.2 us)
Async XLA Ops:
  6.5 14.6 %copy-start = (bf16[320,256]{1,0:T(8,128)(2,1)S(1)}, bf16[320,256]{1,0:T(8,128)(2,1)}, u32[]{:S(2)}) copy-start(bf16[320,256]{1,0:T(8,128)(2,1)} %param.12) | copy-start | bytes 491524
  6.5 14.6 %copy-start.2 = (f32[256]{0:T(256)S(1)}, f32[256]{0:T(256)}, u32[]{:S(2)}) copy-start(f32[256]{0:T(256)} %param.16) | copy-start | bytes 3076
  6.5 53.7 %all-gather.4.cloned.1.call-start = ((), (), s32[]{:S(2)}) async-start(), calls=%async_computation.1 | async-start | bytes 1474560 | tf_op jit(solution)/shard_map/all_gather | solution.py:96
  17.9 85.2 %all-gather.6.cloned.1.call-start = ((), (), s32[]{:S(2)}) async-start(), calls=%async_computation.2 | async-start | bytes 1474560 | tf_op jit(solution)/shard_map/all_gather | solution.py:97
  19.6 139.5 %all-gather.8.cloned.1.call-start = ((), (), s32[]{:S(2)}) async-start(), calls=%async_computation.3 | async-start | bytes 2949120 | tf_op jit(solution)/shard_map/all_gather | solution.py:105
  20.4 180.6 %reduce-scatter.2.cloned.1.call-start = ((), (), s32[]{:S(2)}) async-start(), calls=%async_computation.4 | async-start | bytes 4096000 | tf_op jit(solution)/shard_map/reduce_scatter | solution.py:108
  163.7 37.3 %copy-start.1 = (f32[1280]{0:T(1024)S(1)}, f32[1280]{0:T(1024)}, u32[]{:S(2)}) copy-start(f32[1280]{0:T(1024)} %param.18) | copy-start | bytes 15364
Sparse Core Ops, SparseCore 0:
  18.1 42.1 all-gather.3
  62.4 40.6 all-gather.5
  105.3 53.7 all-gather.7
  163.9 37.0 reduce-scatter.1
where the time goes:
time: 210 us
  waiting for transfers between devices  139 us (66%)
  matrix products  16.4 us (8%)
  other arithmetic  15.6 us (7%)
  between operations  13.8 us (7%)
  local copies, waits for them, and re-layouts  12.6 us (6%)
  blocking collectives  8.4 us (4%)
  loops' own time  3.33 us (2%)
    all_gather x1, waiting for transfers between devices, local(): lax.all_gather(value_heads, 'seq', axis=0, tiled=True)  42.9 us
    all_gather x1, waiting for transfers between devices, local(): lax.all_gather(key_heads, 'seq', axis=0, tiled=True)  39 us
    reduce_scatter x1, waiting for transfers between devices, local(): lax.psum_scatter(terms.astype(jnp.bfloat16), ('head', 'enc'), scatter_dim...  37.3 us
    all_gather x1, waiting for transfers between devices, local(): lax.all_gather(out_weight, 'seq', axis=1, tiled=True)  19.6 us
    dynamic_slice x10, local copies, waits for them, and re-layouts, absorb_blocks(): lax.scan(absorb_block, carried, (numbers, key_blocks, value_blocks))  10.3 us
    dot_general x5, matrix products, absorb(): jnp.einsum('hqk,khd->hqd', weights.astype(jnp.bfloat16), value_block, pre...  9.54 us
    psum x1, blocking collectives, local(): lax.psum((query_squares, key_squares), ('head', 'enc'))  8.4 us
    add x5, other arithmetic, absorb(): running_mass = running_mass * factor + jnp.sum(weights, axis=2)  5.79 us
  transfers between devices with their start and end apart: 4, of which 4 were waited for; matrix products, arithmetic and copies ran while one was open for 17% of the time, Pallas kernels for 0%

commit v1 on v0

--- a/solution.py
+++ b/solution.py
@@ -1,6 +1,8 @@
 import jax
 import jax.numpy as jnp
 from jax import lax
+from jax.experimental import pallas as pl
+from jax.experimental.pallas import tpu as pltpu
 from jax.sharding import PartitionSpec as P
 
 HEAD_DIM = 128
@@ -111,6 +113,295 @@
     return (gate[None, :] * summed).astype(jnp.bfloat16)
 
 
+def fused_kernel(
+    limit_ref, q_ref, k_ref, v_ref, w_ref, qg_ref, kg_ref, gate_ref, out_ref,
+    sums, kv_send, kv_all, q_send, q_both, w_line, w_all, att_send, att_all,
+    sums_ss, sums_rs, mir_ss, mir_rs, kv_ss, kv_rs, wl_ss, wl_rs, w2_ss, w2_rs,
+    am_ss, a_ss, a_rs,
+):
+    seq_size = lax.axis_size("seq")
+    enc_size = lax.axis_size("enc")
+    groups = lax.axis_size("head") * enc_size
+    rows = q_ref.shape[0]
+    half = seq_size // 2
+    inner = seq_size // groups
+    outer = seq_size // inner
+    outer_half = outer // 2
+    feature_count = q_ref.shape[1] * groups
+    s = lax.axis_index("seq")
+    g = lax.axis_index("head") * enc_size + lax.axis_index("enc")
+    head = s // half
+    place = s % half
+    mirror = (s + half) % seq_size
+    a, b = s // inner, s % inner
+    a_mirror = (a + outer_half) % outer
+    a_base = (a // outer_half) * outer_half
+
+    def where_is(seq_index, group):
+        return (seq_index, group // enc_size, group % enc_size)
+
+    def send(src, dst, send_sem, recv_sem, seq_index, group):
+        pltpu.make_async_remote_copy(
+            src_ref=src, dst_ref=dst, send_sem=send_sem, recv_sem=recv_sem,
+            device_id=where_is(seq_index, group), device_id_type=pl.DeviceIdType.MESH,
+        ).start()
+
+    def wait(ref, sem):
+        pltpu.make_async_copy(ref, ref, sem).wait()
+
+    def group_peer(r):
+        return (g + r) % groups
+
+    def half_peer(r):
+        return head * half + (place + r) % half
+
+    def line_peer(r):
+        return a_base + (a - a_base + r) % outer_half
+
+    barrier = pltpu.get_barrier_semaphore()
+    peers = []
+    for rb in range(inner):
+        for r in range(groups):
+            if rb or r:
+                peers.append((a * inner + (b + rb) % inner, group_peer(r)))
+    for ra in range(outer_half):
+        for rb in range(inner):
+            if ra:
+                peers.append((line_peer(ra) * inner + (b + rb) % inner, g))
+    peers.append((mirror, g))
+    for peer in peers:
+        pl.semaphore_signal(
+            barrier, inc=1, device_id=where_is(*peer), device_id_type=pl.DeviceIdType.MESH
+        )
+    pl.semaphore_wait(barrier, len(peers))
+
+    def spread_piece(src, slot, x):
+        for rb in range(inner):
+            target = a * inner + (b + rb) % inner
+            if rb == 0:
+                @pl.when(x == g)
+                def _():
+                    pltpu.make_async_copy(src, w_all.at[b, g], w2_rs.at[b, g]).start()
+
+                @pl.when(x != g)
+                def _():
+                    send(src, w_all.at[b, g], w2_ss.at[slot, rb], w2_rs.at[b, g], target, x)
+            else:
+                send(src, w_all.at[b, g], w2_ss.at[slot, rb], w2_rs.at[b, g], target, x)
+
+    spread_piece(w_ref, 0, a)
+
+    ones = jnp.ones((8, q_ref.shape[1]), jnp.float32)
+
+    def row_sums(ref):
+        value = ref[...].astype(jnp.float32)
+        return lax.dot_general(
+            ones, value * value, (((1,), (1,)), ((), ())),
+            precision=lax.Precision.HIGHEST, preferred_element_type=jnp.float32,
+        )
+
+    sums[g, 0:8, :] = row_sums(q_ref)
+    sums[g, 8:16, :] = row_sums(k_ref)
+    for r in range(1, groups):
+        send(sums.at[g], sums.at[g], sums_ss.at[r], sums_rs.at[g], s, group_peer(r))
+    for r in range(1, groups):
+        wait(sums.at[group_peer(r)], sums_rs.at[group_peer(r)])
+    total = sums[0]
+    for r in range(1, groups):
+        total = total + sums[r]
+    eighth = jnp.full((8, HEAD_DIM), 0.125, jnp.float32)
+
+    def inverse(row_block):
+        column = lax.dot_general(
+            row_block, eighth, (((0,), (0,)), ((), ())),
+            precision=lax.Precision.HIGHEST, preferred_element_type=jnp.float32,
+        )
+        return lax.rsqrt(column / feature_count + epsilon)
+
+    q_inverse = inverse(total[0:8])
+    k_inverse = inverse(total[8:16])
+
+    def normed(ref, factor, gain, which):
+        columns = pl.ds(pl.multiple_of(which * HEAD_DIM, HEAD_DIM), HEAD_DIM)
+        return (ref[:, columns].astype(jnp.float32) * factor * gain[:, columns]).astype(
+            jnp.bfloat16
+        )
+
+    def plain(ref, which):
+        return ref[:, pl.ds(pl.multiple_of(which * HEAD_DIM, HEAD_DIM), HEAD_DIM)]
+
+    kv_send[0] = normed(k_ref, k_inverse, kg_ref, 1 - head)
+    kv_send[1] = plain(v_ref, 1 - head)
+    send(kv_send, kv_all.at[s], mir_ss.at[0], kv_rs.at[s], mirror, g)
+    q_send[...] = normed(q_ref, q_inverse, qg_ref, 1 - head)
+    send(q_send, q_both.at[0], mir_ss.at[1], mir_rs, mirror, g)
+    kv_all[s, 0] = normed(k_ref, k_inverse, kg_ref, head)
+    kv_all[s, 1] = plain(v_ref, head)
+    for r in range(1, half):
+        send(kv_all.at[s], kv_all.at[s], kv_ss.at[0, r], kv_rs.at[s], half_peer(r), g)
+    send(w_ref, w_line.at[a], wl_ss.at[0, 0], wl_rs.at[a], mirror, g)
+    for r in range(1, outer_half):
+        send(w_ref, w_line.at[a], wl_ss.at[0, r], wl_rs.at[a], line_peer(r) * inner + b, g)
+    q_both[1] = normed(q_ref, q_inverse, qg_ref, head)
+
+    wait(kv_all.at[mirror], kv_rs.at[mirror])
+    for r in range(1, half):
+        send(
+            kv_all.at[mirror], kv_all.at[mirror], kv_ss.at[1, r], kv_rs.at[mirror],
+            half_peer(r), g,
+        )
+    for r in range(1, outer_half):
+        x = line_peer(r)
+        wait(w_line.at[x], wl_rs.at[x])
+        spread_piece(w_line.at[x], 1 + r, x)
+    wait(w_line.at[a_mirror], wl_rs.at[a_mirror])
+    for r in range(1, outer_half):
+        send(
+            w_line.at[a_mirror], w_line.at[a_mirror], wl_ss.at[1, r], wl_rs.at[a_mirror],
+            line_peer(r) * inner + b, g,
+        )
+    spread_piece(w_line.at[a_mirror], 1, a_mirror)
+
+    for r in range(1, half):
+        for block in (half_peer(r), (half_peer(r) + half) % seq_size):
+            wait(kv_all.at[block], kv_rs.at[block])
+    wait(q_both.at[0], mir_rs)
+
+    limit = limit_ref[0]
+    scale_factor = HEAD_DIM ** (-0.5)
+    key_count = seq_size * rows
+
+    def attend(query):
+        keys_flat = kv_all[:, 0].reshape(key_count, HEAD_DIM)
+        values_flat = kv_all[:, 1].reshape(key_count, HEAD_DIM)
+        scores = lax.dot_general(
+            query, keys_flat, (((1,), (1,)), ((), ())), preferred_element_type=jnp.float32
+        ) * scale_factor
+        position = lax.broadcasted_iota(jnp.int32, scores.shape, 1)
+        masked = jnp.where(position < limit, scores, lowest_score)
+        weights = jnp.exp(masked - jnp.max(masked, axis=1, keepdims=True))
+        mass = jnp.sum(weights, axis=1, keepdims=True)
+        mixed = jnp.dot(
+            weights.astype(jnp.bfloat16), values_flat, preferred_element_type=jnp.float32
+        )
+        return (mixed / mass).astype(jnp.bfloat16)
+
+    att_send[...] = attend(q_both[0])
+    send(att_send, att_all.at[g, head], am_ss, a_rs.at[g, head], mirror, g)
+    for r in range(1, outer_half):
+        x = (line_peer(r) + outer_half) % outer
+        wait(w_line.at[x], wl_rs.at[x])
+        spread_piece(w_line.at[x], outer_half + r, x)
+    att_all[g, head] = attend(q_both[1])
+    for r in range(1, groups):
+        send(
+            att_all.at[g, head], att_all.at[g, head], a_ss.at[0, r], a_rs.at[g, head],
+            s, group_peer(r),
+        )
+    other = 1 - head
+    wait(att_all.at[g, other], a_rs.at[g, other])
+    for r in range(1, groups):
+        send(
+            att_all.at[g, other], att_all.at[g, other], a_ss.at[1, r], a_rs.at[g, other],
+            s, group_peer(r),
+        )
+    for r in range(1, groups):
+        for which in range(2):
+            wait(att_all.at[group_peer(r), which], a_rs.at[group_peer(r), which])
+
+    width = w_ref.shape[1]
+    for piece in range(inner):
+        summed = None
+        for group in range(groups):
+            wait(w_all.at[piece, group], w2_rs.at[piece, group])
+            lhs = jnp.concatenate([att_all[group, 0], att_all[group, 1]], axis=1)
+            term = jnp.dot(lhs, w_all[piece, group], preferred_element_type=jnp.float32)
+            term = term.astype(jnp.bfloat16).astype(jnp.float32)
+            summed = term if summed is None else summed + term
+        columns = slice(piece * width, (piece + 1) * width)
+        out_ref[:, columns] = (gate_ref[:, columns] * summed).astype(jnp.bfloat16)
+
+    for r in range(1, groups):
+        wait(sums.at[g], sums_ss.at[r])
+    wait(kv_send, mir_ss.at[0])
+    wait(q_send, mir_ss.at[1])
+    for turn in range(2):
+        for r in range(1, half):
+            wait(kv_all.at[s], kv_ss.at[turn, r])
+        for r in range(1, outer_half):
+            wait(w_ref, wl_ss.at[turn, r])
+        for r in range(1, groups):
+            wait(att_send, a_ss.at[turn, r])
+    wait(w_ref, wl_ss.at[0, 0])
+    wait(att_send, am_ss)
+    pieces = [(0, a), (1, a_mirror)]
+    for r in range(1, outer_half):
+        pieces.append((1 + r, line_peer(r)))
+        pieces.append((outer_half + r, (line_peer(r) + outer_half) % outer))
+    for slot, x in pieces:
+        for rb in range(inner):
+            if rb == 0:
+                @pl.when(x != g)
+                def _():
+                    wait(w_ref, w2_ss.at[slot, rb])
+            else:
+                wait(w_ref, w2_ss.at[slot, rb])
+
+
+def fused(queries, keys, values, out_weight, q_gain, k_gain, gate, valid_count):
+    seq_size = lax.axis_size("seq")
+    groups = lax.axis_size("head") * lax.axis_size("enc")
+    inner = seq_size // groups
+    outer = seq_size // inner
+    rows, local_width = queries.shape
+    depth, width = out_weight.shape
+    half = seq_size // 2
+    outer_half = outer // 2
+    bf16, f32 = jnp.bfloat16, jnp.float32
+    dma = pltpu.SemaphoreType.DMA
+    vmem = pl.BlockSpec(memory_space=pltpu.VMEM)
+    return pl.pallas_call(
+        fused_kernel,
+        out_shape=jax.ShapeDtypeStruct((rows, width * inner), bf16),
+        in_specs=[pl.BlockSpec(memory_space=pltpu.SMEM)] + [vmem] * 7,
+        out_specs=vmem,
+        scratch_shapes=[
+            pltpu.VMEM((groups, 16, rows), f32),
+            pltpu.VMEM((2, rows, HEAD_DIM), bf16),
+            pltpu.VMEM((seq_size, 2, rows, HEAD_DIM), bf16),
+            pltpu.VMEM((rows, HEAD_DIM), bf16),
+            pltpu.VMEM((2, rows, HEAD_DIM), bf16),
+            pltpu.VMEM((outer, depth, width), bf16),
+            pltpu.VMEM((inner, groups, depth, width), bf16),
+            pltpu.VMEM((rows, HEAD_DIM), bf16),
+            pltpu.VMEM((groups, 2, rows, HEAD_DIM), bf16),
+            dma((groups,)), dma((groups,)),
+            dma((2,)), dma,
+            dma((2, half)), dma((seq_size,)),
+            dma((2, outer_half)), dma((outer,)),
+            dma((outer, inner)), dma((inner, groups)),
+            dma, dma((2, groups)), dma((groups, 2)),
+        ],
+        compiler_params=pltpu.CompilerParams(
+            collective_id=0, has_side_effects=True, vmem_limit_bytes=56 * 2**20
+        ),
+    )(
+        valid_count, queries, keys, values, out_weight,
+        q_gain[None, :], k_gain[None, :], gate[None, :],
+    )
+
+
+def one_kernel_fits(mesh, queries, out_weight):
+    sizes = mesh.shape
+    seq_size, groups = sizes["seq"], sizes["head"] * sizes["enc"]
+    return (
+        seq_size % groups == 0
+        and groups % 2 == 0
+        and queries.shape[1] == 2 * groups * HEAD_DIM
+        and (out_weight.shape[1] // seq_size) % HEAD_DIM == 0
+    )
+
+
 def solution(mesh):
     placed = (
         P("seq", ("head", "enc")),
@@ -122,6 +413,12 @@
         P(("head", "enc")),
         P(),
     )
-    return jax.shard_map(
-        local, mesh=mesh, in_specs=placed, out_specs=P("seq", ("head", "enc")), check_vma=False
-    )
+
+    def run(*arguments):
+        body = fused if one_kernel_fits(mesh, arguments[0], arguments[3]) else local
+        return jax.shard_map(
+            body, mesh=mesh, in_specs=placed, out_specs=P("seq", ("head", "enc")),
+            check_vma=False,
+        )(*arguments)
+
+    return run

time: 210 us -> 99.5 us (0.47)
  the two profiles are of different devices: /device:TPU:0 before, /device:TPU:19 now
where the time goes in v1:
time: 99.5 us; the launch traced here: 99.3 us
  Pallas kernels  95.2 us (96%)
  local copies, waits for them, and re-layouts  3.38 us (3%)
    pallas_call x1, Pallas kernels, fused(): pl.pallas_call(fused_kernel, out_shape=jax.ShapeDtypeStruct((rows, width...  95.2 us
    unnamed x1, local copies, waits for them, and re-layouts  2.09 us

profile of v1, /device:TPU:19, one launch (start us, length us, event | category | flops | bytes accessed | tf_op | source)
XLA Modules:
  0.0 99.3 jit_solution(17575685217352520810)
XLA Ops:
  0.7 1.3 %broadcast_in_dim.11.gate_ref = f32[1,1280]{1,0:T(1,128)} reshape(f32[1280]{0:T(1024)} %param.14) | data formatting | bytes 10240 | tf_op jit(solution)/shard_map/broadcast_in_dim | solution.py:390
  1.9 95.2 %shard_map.82 = bf16[320,1280]{1,0:T(8,128)(2,1)} custom-call(s32[1]{0:T(128)S(6)} %copy.10.limit_ref, bf16[320,256]{1,0:T(8,128)(2,1)} %q_ref.1, bf16[320,256]{1,0:T(8,128)(2,1)} %k_ref.1, bf16[320,256]{1,0:T(8,128)(2,1)} %v_ref.1, bf16[256,640]{1,0:T(8,128)(2,1)} %w_ref.1, f32[1,256]{1,0:T(1,128)} %bitcast.2, f32[1,256]{1,0:T(1,128)} %bitcast.3, ...), custom_call_target="tpu_custom_call" | custom-call | tf_op jit(solution)/shard_map/pallas_call | solution.py:363
  97.2 2.1 %copy.11 = bf16[320,1280]{1,0:T(8,128)(2,1)} copy(bf16[320,1280]{1,0:T(8,128)(2,1)} %shard_map.82) | data formatting | bytes 1638400

commit v2 on v1

--- a/solution.py
+++ b/solution.py
@@ -115,26 +115,26 @@
 
 def fused_kernel(
     limit_ref, q_ref, k_ref, v_ref, w_ref, qg_ref, kg_ref, gate_ref, out_ref,
-    sums, kv_send, kv_all, q_send, q_both, w_line, w_all, att_send, att_all,
-    sums_ss, sums_rs, mir_ss, mir_rs, kv_ss, kv_rs, wl_ss, wl_rs, w2_ss, w2_rs,
-    am_ss, a_ss, a_rs,
+    sums, kv_send, kv_all, q_send, q_all, w_line, w_all, att_send, att_all,
+    sums_ss, sums_rs, kv1_ss, q1_ss, q_rs, kv2_ss, kv3_ss, kv_rs, wl_ss, wl_rs, w2_ss, w2_rs,
+    a1_ss, a2_ss, a_rs,
 ):
     seq_size = lax.axis_size("seq")
     enc_size = lax.axis_size("enc")
     groups = lax.axis_size("head") * enc_size
     rows = q_ref.shape[0]
-    half = seq_size // 2
     inner = seq_size // groups
     outer = seq_size // inner
     outer_half = outer // 2
+    shares = outer // enc_size
     feature_count = q_ref.shape[1] * groups
     s = lax.axis_index("seq")
-    g = lax.axis_index("head") * enc_size + lax.axis_index("enc")
-    head = s // half
-    place = s % half
-    mirror = (s + half) % seq_size
+    e = lax.axis_index("enc")
+    h = lax.axis_index("head")
+    g = h * enc_size + e
     a, b = s // inner, s % inner
     a_mirror = (a + outer_half) % outer
+    mirror = a_mirror * inner + b
     a_base = (a // outer_half) * outer_half
 
     def where_is(seq_index, group):
@@ -151,9 +151,6 @@
 
     def group_peer(r):
         return (g + r) % groups
-
-    def half_peer(r):
-        return head * half + (place + r) % half
 
     def line_peer(r):
         return a_base + (a - a_base + r) % outer_half
@@ -164,11 +161,9 @@
         for r in range(groups):
             if rb or r:
                 peers.append((a * inner + (b + rb) % inner, group_peer(r)))
-    for ra in range(outer_half):
-        for rb in range(inner):
-            if ra:
-                peers.append((line_peer(ra) * inner + (b + rb) % inner, g))
-    peers.append((mirror, g))
+    for ra in range(1, outer):
+        for re in range(enc_size):
+            peers.append((((a + ra) % outer) * inner + b, h * enc_size + re))
     for peer in peers:
         pl.semaphore_signal(
             barrier, inc=1, device_id=where_is(*peer), device_id_type=pl.DeviceIdType.MESH
@@ -189,8 +184,6 @@
             else:
                 send(src, w_all.at[b, g], w2_ss.at[slot, rb], w2_rs.at[b, g], target, x)
 
-    spread_piece(w_ref, 0, a)
-
     ones = jnp.ones((8, q_ref.shape[1]), jnp.float32)
 
     def row_sums(ref):
@@ -204,6 +197,11 @@
     sums[g, 8:16, :] = row_sums(k_ref)
     for r in range(1, groups):
         send(sums.at[g], sums.at[g], sums_ss.at[r], sums_rs.at[g], s, group_peer(r))
+    for r in range(1, outer_half):
+        send(w_ref, w_line.at[a], wl_ss.at[0, r], wl_rs.at[a], line_peer(r) * inner + b, g)
+    send(w_ref, w_line.at[a], wl_ss.at[0, 0], wl_rs.at[a], mirror, g)
+    spread_piece(w_ref, 0, a)
+
     for r in range(1, groups):
         wait(sums.at[group_peer(r)], sums_rs.at[group_peer(r)])
     total = sums[0]
@@ -230,30 +228,70 @@
     def plain(ref, which):
         return ref[:, pl.ds(pl.multiple_of(which * HEAD_DIM, HEAD_DIM), HEAD_DIM)]
 
-    kv_send[0] = normed(k_ref, k_inverse, kg_ref, 1 - head)
-    kv_send[1] = plain(v_ref, 1 - head)
-    send(kv_send, kv_all.at[s], mir_ss.at[0], kv_rs.at[s], mirror, g)
-    q_send[...] = normed(q_ref, q_inverse, qg_ref, 1 - head)
-    send(q_send, q_both.at[0], mir_ss.at[1], mir_rs, mirror, g)
-    kv_all[s, 0] = normed(k_ref, k_inverse, kg_ref, head)
-    kv_all[s, 1] = plain(v_ref, head)
-    for r in range(1, half):
-        send(kv_all.at[s], kv_all.at[s], kv_ss.at[0, r], kv_rs.at[s], half_peer(r), g)
-    send(w_ref, w_line.at[a], wl_ss.at[0, 0], wl_rs.at[a], mirror, g)
-    for r in range(1, outer_half):
-        send(w_ref, w_line.at[a], wl_ss.at[0, r], wl_rs.at[a], line_peer(r) * inner + b, g)
-    q_both[1] = normed(q_ref, q_inverse, qg_ref, head)
-
-    wait(kv_all.at[mirror], kv_rs.at[mirror])
-    for r in range(1, half):
-        send(
-            kv_all.at[mirror], kv_all.at[mirror], kv_ss.at[1, r], kv_rs.at[mirror],
-            half_peer(r), g,
-        )
+    catcher = a % enc_size
+    for i in range(2):
+        plane = e * 2 + i
+        local_turn = jnp.logical_and(plane == a, catcher == e)
+        target = plane * inner + b
+        target_group = h * enc_size + catcher
+        kv_send[i, 0] = normed(k_ref, k_inverse, kg_ref, i)
+        kv_send[i, 1] = plain(v_ref, i)
+        q_send[i] = normed(q_ref, q_inverse, qg_ref, i)
+
+        @pl.when(local_turn)
+        def _():
+            pltpu.make_async_copy(kv_send.at[i], kv_all.at[s], kv_rs.at[s]).start()
+            pltpu.make_async_copy(
+                q_send.at[i], q_all.at[a // enc_size], q_rs.at[a // enc_size]
+            ).start()
+
+        @pl.when(jnp.logical_not(local_turn))
+        def _():
+            send(
+                kv_send.at[i], kv_all.at[s], kv1_ss.at[i], kv_rs.at[s], target, target_group
+            )
+            send(
+                q_send.at[i], q_all.at[a // enc_size], q1_ss.at[i], q_rs.at[a // enc_size],
+                target, target_group,
+            )
+
     for r in range(1, outer_half):
         x = line_peer(r)
         wait(w_line.at[x], wl_rs.at[x])
         spread_piece(w_line.at[x], 1 + r, x)
+
+    def share_of(turn):
+        return (a // enc_size + turn) % shares
+
+    def block_at(turn, core, column):
+        return (share_of(turn) * enc_size + core) * inner + column
+
+    def pass_on(turn):
+        block = block_at(turn, e, b)
+        wait(kv_all.at[block], kv_rs.at[block])
+        for rb in range(1, inner):
+            send(
+                kv_all.at[block], kv_all.at[block], kv2_ss.at[turn, enc_size + rb],
+                kv_rs.at[block], a * inner + (b + rb) % inner, g,
+            )
+        for re in range(1, enc_size):
+            send(
+                kv_all.at[block], kv_all.at[block], kv2_ss.at[turn, re], kv_rs.at[block],
+                s, h * enc_size + (e + re) % enc_size,
+            )
+
+    def pass_across(turn):
+        for rb in range(1, inner):
+            block = block_at(turn, e, (b + rb) % inner)
+            wait(kv_all.at[block], kv_rs.at[block])
+            for re in range(1, enc_size):
+                send(
+                    kv_all.at[block], kv_all.at[block], kv3_ss.at[turn, rb, re],
+                    kv_rs.at[block], s, h * enc_size + (e + re) % enc_size,
+                )
+
+    for turn in range(shares):
+        pass_on(turn)
     wait(w_line.at[a_mirror], wl_rs.at[a_mirror])
     for r in range(1, outer_half):
         send(
@@ -261,11 +299,15 @@
             line_peer(r) * inner + b, g,
         )
     spread_piece(w_line.at[a_mirror], 1, a_mirror)
-
-    for r in range(1, half):
-        for block in (half_peer(r), (half_peer(r) + half) % seq_size):
-            wait(kv_all.at[block], kv_rs.at[block])
-    wait(q_both.at[0], mir_rs)
+    for turn in range(shares):
+        pass_across(turn)
+    for turn in range(shares):
+        for re in range(1, enc_size):
+            for rb in range(inner):
+                block = block_at(turn, (e + re) % enc_size, (b + rb) % inner)
+                wait(kv_all.at[block], kv_rs.at[block])
+    for share in range(shares):
+        wait(q_all.at[share], q_rs.at[share])
 
     limit = limit_ref[0]
     scale_factor = HEAD_DIM ** (-0.5)
@@ -286,28 +328,53 @@
         )
         return (mixed / mass).astype(jnp.bfloat16)
 
-    att_send[...] = attend(q_both[0])
-    send(att_send, att_all.at[g, head], am_ss, a_rs.at[g, head], mirror, g)
-    for r in range(1, outer_half):
-        x = (line_peer(r) + outer_half) % outer
-        wait(w_line.at[x], wl_rs.at[x])
-        spread_piece(w_line.at[x], outer_half + r, x)
-    att_all[g, head] = attend(q_both[1])
-    for r in range(1, groups):
-        send(
-            att_all.at[g, head], att_all.at[g, head], a_ss.at[0, r], a_rs.at[g, head],
-            s, group_peer(r),
-        )
-    other = 1 - head
-    wait(att_all.at[g, other], a_rs.at[g, other])
-    for r in range(1, groups):
-        send(
-            att_all.at[g, other], att_all.at[g, other], a_ss.at[1, r], a_rs.at[g, other],
-            s, group_peer(r),
-        )
-    for r in range(1, groups):
-        for which in range(2):
-            wait(att_all.at[group_peer(r), which], a_rs.at[group_peer(r), which])
+    mine = h * enc_size + a // 2
+    which = a % 2
+    for turn in range(shares):
+        share = share_of(turn + 1)
+        plane = share * enc_size + e
+        att_send[turn] = attend(q_all[share])
+
+        @pl.when(plane == a)
+        def _():
+            pltpu.make_async_copy(
+                att_send.at[turn], att_all.at[mine, which], a_rs.at[mine, which]
+            ).start()
+
+        @pl.when(plane != a)
+        def _():
+            send(
+                att_send.at[turn], att_all.at[mine, which], a1_ss.at[turn],
+                a_rs.at[mine, which], plane * inner + b, g,
+            )
+
+        if turn == 0:
+            for r in range(1, outer_half):
+                x = (line_peer(r) + outer_half) % outer
+                wait(w_line.at[x], wl_rs.at[x])
+                spread_piece(w_line.at[x], outer_half + r, x)
+
+    @pl.when(e == catcher)
+    def _():
+        for ra in range(outer):
+            plane = (a + ra) % outer
+            group, i = h * enc_size + plane // 2, plane % 2
+            wait(att_all.at[group, i], a_rs.at[group, i])
+            for r in range(1, groups):
+                send(
+                    att_all.at[group, i], att_all.at[group, i], a2_ss.at[ra, r],
+                    a_rs.at[group, i], s, group_peer(r),
+                )
+        for rh in range(enc_size, groups):
+            group = (h * enc_size + rh) % groups
+            for i in range(2):
+                wait(att_all.at[group, i], a_rs.at[group, i])
+
+    @pl.when(e != catcher)
+    def _():
+        for group in range(groups):
+            for i in range(2):
+                wait(att_all.at[group, i], a_rs.at[group, i])
 
     width = w_ref.shape[1]
     for piece in range(inner):
@@ -319,21 +386,37 @@
             term = term.astype(jnp.bfloat16).astype(jnp.float32)
             summed = term if summed is None else summed + term
         columns = slice(piece * width, (piece + 1) * width)
-        out_ref[:, columns] = (gate_ref[:, columns] * summed).astype(jnp.bfloat16)
+        out_ref[:, columns] = (gate_ref[columns][None, :] * summed).astype(jnp.bfloat16)
 
     for r in range(1, groups):
         wait(sums.at[g], sums_ss.at[r])
-    wait(kv_send, mir_ss.at[0])
-    wait(q_send, mir_ss.at[1])
+    for i in range(2):
+        @pl.when(jnp.logical_not(jnp.logical_and(e * 2 + i == a, catcher == e)))
+        def _():
+            wait(kv_send.at[i], kv1_ss.at[i])
+            wait(q_send.at[i], q1_ss.at[i])
+    for turn in range(shares):
+        for re in range(1, enc_size):
+            wait(kv_send.at[0], kv2_ss.at[turn, re])
+        for rb in range(1, inner):
+            wait(kv_send.at[0], kv2_ss.at[turn, enc_size + rb])
+            for re in range(1, enc_size):
+                wait(kv_send.at[0], kv3_ss.at[turn, rb, re])
+
+        @pl.when(share_of(turn + 1) * enc_size + e != a)
+        def _():
+            wait(att_send.at[turn], a1_ss.at[turn])
+
+    @pl.when(e == catcher)
+    def _():
+        for ra in range(outer):
+            for r in range(1, groups):
+                wait(att_send.at[0], a2_ss.at[ra, r])
+
     for turn in range(2):
-        for r in range(1, half):
-            wait(kv_all.at[s], kv_ss.at[turn, r])
         for r in range(1, outer_half):
             wait(w_ref, wl_ss.at[turn, r])
-        for r in range(1, groups):
-            wait(att_send, a_ss.at[turn, r])
     wait(w_ref, wl_ss.at[0, 0])
-    wait(att_send, am_ss)
     pieces = [(0, a), (1, a_mirror)]
     for r in range(1, outer_half):
         pieces.append((1 + r, line_peer(r)))
@@ -355,7 +438,8 @@
     outer = seq_size // inner
     rows, local_width = queries.shape
     depth, width = out_weight.shape
-    half = seq_size // 2
+    enc_size = lax.axis_size("enc")
+    shares = outer // enc_size
     outer_half = outer // 2
     bf16, f32 = jnp.bfloat16, jnp.float32
     dma = pltpu.SemaphoreType.DMA
@@ -367,27 +451,27 @@
         out_specs=vmem,
         scratch_shapes=[
             pltpu.VMEM((groups, 16, rows), f32),
+            pltpu.VMEM((2, 2, rows, HEAD_DIM), bf16),
+            pltpu.VMEM((seq_size, 2, rows, HEAD_DIM), bf16),
             pltpu.VMEM((2, rows, HEAD_DIM), bf16),
-            pltpu.VMEM((seq_size, 2, rows, HEAD_DIM), bf16),
-            pltpu.VMEM((rows, HEAD_DIM), bf16),
-            pltpu.VMEM((2, rows, HEAD_DIM), bf16),
+            pltpu.VMEM((shares, rows, HEAD_DIM), bf16),
             pltpu.VMEM((outer, depth, width), bf16),
             pltpu.VMEM((inner, groups, depth, width), bf16),
-            pltpu.VMEM((rows, HEAD_DIM), bf16),
+            pltpu.VMEM((shares, rows, HEAD_DIM), bf16),
             pltpu.VMEM((groups, 2, rows, HEAD_DIM), bf16),
             dma((groups,)), dma((groups,)),
-            dma((2,)), dma,
-            dma((2, half)), dma((seq_size,)),
+            dma((2,)), dma((2,)), dma((shares,)),
+            dma((shares, enc_size + inner)), dma((shares, inner, enc_size)), dma((seq_size,)),
             dma((2, outer_half)), dma((outer,)),
             dma((outer, inner)), dma((inner, groups)),
-            dma, dma((2, groups)), dma((groups, 2)),
+            dma((shares,)), dma((outer, groups)), dma((groups, 2)),
         ],
         compiler_params=pltpu.CompilerParams(
             collective_id=0, has_side_effects=True, vmem_limit_bytes=56 * 2**20
         ),
     )(
         valid_count, queries, keys, values, out_weight,
-        q_gain[None, :], k_gain[None, :], gate[None, :],
+        q_gain[None, :], k_gain[None, :], gate,
     )
 
 
@@ -397,6 +481,7 @@
     return (
         seq_size % groups == 0
         and groups % 2 == 0
+        and seq_size // (seq_size // groups) == 2 * sizes["enc"]
         and queries.shape[1] == 2 * groups * HEAD_DIM
         and (out_weight.shape[1] // seq_size) % HEAD_DIM == 0
     )

time: 99.5 us -> 74.5 us (0.75)
  the two profiles are of different devices: /device:TPU:19 before, /device:TPU:5 now
where the time goes in v2:
time: 74.5 us; the launch traced here: 74.3 us
  Pallas kernels  71.6 us (96%)
  local copies, waits for them, and re-layouts  2.09 us (3%)
    pallas_call x1, Pallas kernels, fused(): pl.pallas_call(fused_kernel, out_shape=jax.ShapeDtypeStruct((rows, width...  71.6 us
    unnamed x1, local copies, waits for them, and re-layouts  2.09 us

profile of v2, /device:TPU:5, one launch (start us, length us, event | category | flops | bytes accessed | tf_op | source)
XLA Modules:
  0.0 74.3 jit_solution(3336685499884050998)
XLA Ops:
  0.7 71.6 %shard_map.82 = bf16[320,1280]{1,0:T(8,128)(2,1)} custom-call(s32[1]{0:T(128)S(6)} %copy.10.limit_ref, bf16[320,256]{1,0:T(8,128)(2,1)} %q_ref.1, bf16[320,256]{1,0:T(8,128)(2,1)} %k_ref.1, bf16[320,256]{1,0:T(8,128)(2,1)} %v_ref.1, bf16[256,640]{1,0:T(8,128)(2,1)} %w_ref.1, f32[1,256]{1,0:T(1,128)} %bitcast.2, f32[1,256]{1,0:T(1,128)} %bitcast.3, f32[1280]{0:T(1024)} %gate_ref.1), custom_call_target="tpu_custom_call" | custom-call | tf_op jit(solution)/shard_map/pallas_call | solution.py:447
  72.2 2.1 %copy.11 = bf16[320,1280]{1,0:T(8,128)(2,1)} copy(bf16[320,1280]{1,0:T(8,128)(2,1)} %shard_map.82) | data formatting | bytes 1638400

commit v3 on v2

--- a/solution.py
+++ b/solution.py
@@ -116,7 +116,7 @@
 def fused_kernel(
     limit_ref, q_ref, k_ref, v_ref, w_ref, qg_ref, kg_ref, gate_ref, out_ref,
     sums, kv_send, kv_all, q_send, q_all, w_line, w_all, att_send, att_all,
-    sums_ss, sums_rs, kv1_ss, q1_ss, q_rs, kv2_ss, kv3_ss, kv_rs, wl_ss, wl_rs, w2_ss, w2_rs,
+    sums_ss, sums_rs, kv1_ss, q1_ss, q_rs, kv2_ss, kv3_ss, kv_rs, wl_ss, wl_rs, w2_ss, w2_rs, w3_ss,
     a1_ss, a2_ss, a_rs,
 ):
     seq_size = lax.axis_size("seq")
@@ -170,6 +170,20 @@
         )
     pl.semaphore_wait(barrier, len(peers))
 
+    def by_relay(from_head, from_core, to_head):
+        return from_head != to_head
+
+    def relay_pieces():
+        for group in range(groups):
+            @pl.when(by_relay(group // enc_size, group % enc_size, h))
+            def _():
+                wait(w_all.at[b, group], w2_rs.at[b, group])
+                for rb in range(1, inner):
+                    send(
+                        w_all.at[b, group], w_all.at[b, group], w3_ss.at[group, rb],
+                        w2_rs.at[b, group], a * inner + (b + rb) % inner, g,
+                    )
+
     def spread_piece(src, slot, x):
         for rb in range(inner):
             target = a * inner + (b + rb) % inner
@@ -182,7 +196,9 @@
                 def _():
                     send(src, w_all.at[b, g], w2_ss.at[slot, rb], w2_rs.at[b, g], target, x)
             else:
-                send(src, w_all.at[b, g], w2_ss.at[slot, rb], w2_rs.at[b, g], target, x)
+                @pl.when(jnp.logical_not(by_relay(h, e, x // enc_size)))
+                def _():
+                    send(src, w_all.at[b, g], w2_ss.at[slot, rb], w2_rs.at[b, g], target, x)
 
     ones = jnp.ones((8, q_ref.shape[1]), jnp.float32)
 
@@ -301,6 +317,12 @@
     spread_piece(w_line.at[a_mirror], 1, a_mirror)
     for turn in range(shares):
         pass_across(turn)
+    near = g // outer_half == a // outer_half
+
+    @pl.when(near)
+    def _():
+        relay_pieces()
+
     for turn in range(shares):
         for re in range(1, enc_size):
             for rb in range(inner):
@@ -353,6 +375,10 @@
                 x = (line_peer(r) + outer_half) % outer
                 wait(w_line.at[x], wl_rs.at[x])
                 spread_piece(w_line.at[x], outer_half + r, x)
+
+            @pl.when(jnp.logical_not(near))
+            def _():
+                relay_pieces()
 
     @pl.when(e == catcher)
     def _():
@@ -380,7 +406,14 @@
     for piece in range(inner):
         summed = None
         for group in range(groups):
-            wait(w_all.at[piece, group], w2_rs.at[piece, group])
+            relayed = jnp.logical_and(
+                piece == b, by_relay(group // enc_size, group % enc_size, h)
+            )
+
+            @pl.when(jnp.logical_not(relayed))
+            def _():
+                wait(w_all.at[piece, group], w2_rs.at[piece, group])
+
             lhs = jnp.concatenate([att_all[group, 0], att_all[group, 1]], axis=1)
             term = jnp.dot(lhs, w_all[piece, group], preferred_element_type=jnp.float32)
             term = term.astype(jnp.bfloat16).astype(jnp.float32)
@@ -428,7 +461,14 @@
                 def _():
                     wait(w_ref, w2_ss.at[slot, rb])
             else:
-                wait(w_ref, w2_ss.at[slot, rb])
+                @pl.when(jnp.logical_not(by_relay(h, e, x // enc_size)))
+                def _():
+                    wait(w_ref, w2_ss.at[slot, rb])
+    for group in range(groups):
+        @pl.when(by_relay(group // enc_size, group % enc_size, h))
+        def _():
+            for rb in range(1, inner):
+                wait(w_ref, w3_ss.at[group, rb])
 
 
 def fused(queries, keys, values, out_weight, q_gain, k_gain, gate, valid_count):
@@ -463,7 +503,7 @@
             dma((2,)), dma((2,)), dma((shares,)),
             dma((shares, enc_size + inner)), dma((shares, inner, enc_size)), dma((seq_size,)),
             dma((2, outer_half)), dma((outer,)),
-            dma((outer, inner)), dma((inner, groups)),
+            dma((outer, inner)), dma((inner, groups)), dma((groups, inner)),
             dma((shares,)), dma((outer, groups)), dma((groups, 2)),
         ],
         compiler_params=pltpu.CompilerParams(

time: 74.5 us -> 69.1 us (0.928)
  the two profiles are of different devices: /device:TPU:5 before, /device:TPU:0 now
where the time goes in v3:
time: 69.1 us; the launch traced here: 68.7 us
  Pallas kernels  66 us (96%)
  local copies, waits for them, and re-layouts  2.09 us (3%)
    pallas_call x1, Pallas kernels, fused(): pl.pallas_call(fused_kernel, out_shape=jax.ShapeDtypeStruct((rows, width...  66 us
    unnamed x1, local copies, waits for them, and re-layouts  2.09 us

profile of v3, /device:TPU:0, one launch (start us, length us, event | category | flops | bytes accessed | tf_op | source)
XLA Modules:
  0.0 68.7 jit_solution(7602849430941735912)
XLA Ops:
  0.7 66.0 %shard_map.82 = bf16[320,1280]{1,0:T(8,128)(2,1)} custom-call(s32[1]{0:T(128)S(6)} %copy.10.limit_ref, bf16[320,256]{1,0:T(8,128)(2,1)} %q_ref.1, bf16[320,256]{1,0:T(8,128)(2,1)} %k_ref.1, bf16[320,256]{1,0:T(8,128)(2,1)} %v_ref.1, bf16[256,640]{1,0:T(8,128)(2,1)} %w_ref.1, f32[1,256]{1,0:T(1,128)} %bitcast.2, f32[1,256]{1,0:T(1,128)} %bitcast.3, f32[1280]{0:T(1024)} %gate_ref.1), custom_call_target="tpu_custom_call" | custom-call | tf_op jit(solution)/shard_map/pallas_call | solution.py:487
  66.6 2.1 %copy.11 = bf16[320,1280]{1,0:T(8,128)(2,1)} copy(bf16[320,1280]{1,0:T(8,128)(2,1)} %shard_map.82) | data formatting | bytes 1638400
